TPU v7x, 512 devices: a whole 4x4x16 slice. The times are simulated.
512 devices in a mesh: grp: 16 (over y, x), ctx: 32 (over z, core).
Axes of the slice: x: 4, y: 4, z: 16, core: 2. Of those that a mesh axis runs over, the one named last changes fastest.
Arguments:
- queries: bfloat16 [262144, 1024], P(('grp', 'ctx')), may hold values from -6 to 6
- keys: bfloat16 [262144, 1024], P(('grp', 'ctx')), may hold values from -6 to 6
- values: bfloat16 [262144, 1024], P(('grp', 'ctx')), may hold values from -6 to 6
- level_weights: float32 [13, 8, 262144], P(None, None, ('grp', 'ctx')), may hold values from 0.1 to 1.5
Outputs:
- attended: bfloat16 [262144, 1024], P(('grp', 'ctx'))
All inputs are finite; a program needn't handle non-finite values.
Results may differ from a plain program's by a relative error of at most 0.0095.
Values may be sent and summed in bfloat16 or wider, within the bound.
No kernel may reach another device: no remote copies, remote signals or barrier semaphores. Data moves between devices by JAX's collectives and lax.ppermute only.
A program may use at most 64 MiB of HBM per device.

v0:
```python
import math
import jax
import jax.numpy as jnp
from jax import lax
from jax.sharding import PartitionSpec as P

DK = 128
STRETCH = 64


def from_partner(block, axis, stride):
    count = lax.axis_size(axis)
    route = []
    for low in range(count):
        high = low | 1 << stride
        if high != low and high < count:
            route += [(low, high), (high, low)]
    return lax.ppermute(block, axis, route)


def level_factor(level_num):
    token_count = STRETCH if level_num == 0 else STRETCH * 2 ** (level_num - 1)
    return 1.0 / math.sqrt(DK * token_count)


def local_part(query_matrix, key_matrix, value_matrix, level_rows):
    row_count = query_matrix.shape[0]
    local_bits = (row_count // STRETCH).bit_length() - 1
    position = jnp.arange(row_count, dtype=jnp.int32)
    block_ids = position // STRETCH
    stretch_xor = jnp.bitwise_xor(block_ids[:, None], block_ids[None, :])
    level_ids = jnp.zeros((row_count, row_count), jnp.int32)
    for bit_num in range(local_bits):
        level_ids = level_ids + (stretch_xor >= 2**bit_num).astype(jnp.int32)
    causal = position[:, None] >= position[None, :]
    weight = jnp.zeros((level_rows.shape[1], row_count, row_count), jnp.float32)
    for level_num in range(local_bits + 1):
        picked = jnp.logical_and(level_ids == level_num, causal)
        weight = weight + jnp.where(
            picked[None], (level_rows[level_num] * level_factor(level_num))[:, :, None], 0.0
        )
    scores = jnp.einsum(
        "thk,shk->hts", query_matrix, key_matrix, preferred_element_type=jnp.float32
    )
    weighted = (scores * weight).astype(jnp.bfloat16)
    return jnp.einsum("hts,shv->thv", weighted, value_matrix, preferred_element_type=jnp.float32)


def sibling_weights(piece_rows, self_position, bit_count):
    device_ids = jnp.arange(piece_rows, dtype=jnp.int32)
    columns = []
    for bit_num in range(bit_count):
        own_block = jnp.right_shift(self_position, bit_num)
        member = jnp.logical_and(
            jnp.right_shift(device_ids, bit_num) == own_block - 1, own_block % 2 == 1
        )
        columns.append(member)
    return jnp.stack(columns, axis=1).astype(jnp.bfloat16)


def collect_into(self_position, bit_count, shard_rows):
    selector = sibling_weights(shard_rows.shape[0], self_position, bit_count)
    return jnp.einsum("nl,nhkv->lhkv", selector, shard_rows, preferred_element_type=jnp.float32)


def on_device(queries, keys, values, level_weights):
    row_count = queries.shape[0]
    head_count = level_weights.shape[1]
    head_width = queries.shape[1] // head_count
    query_matrix = queries.reshape(row_count, head_count, head_width)
    key_matrix = keys.reshape(row_count, head_count, head_width)
    value_matrix = values.reshape(row_count, head_count, head_width)
    local_bits = (row_count // STRETCH).bit_length() - 1
    ctx_bits = lax.axis_size("ctx").bit_length() - 1
    grp_bits = lax.axis_size("grp").bit_length() - 1
    ctx_index = lax.axis_index("ctx")
    grp_index = lax.axis_index("grp")
    kv_state = jnp.einsum(
        "pdx,pdo->dxo", key_matrix, value_matrix, preferred_element_type=jnp.float32
    ).astype(jnp.bfloat16)
    siblings = []
    running = kv_state.astype(jnp.float32)
    for bit_num in range(ctx_bits):
        partner = from_partner(running, "ctx", bit_num)
        left_half = jnp.right_shift(ctx_index, bit_num) % 2 == 1
        siblings.append(jnp.where(left_half, partner, 0.0))
        running = running + partner
    group_state = running.astype(jnp.bfloat16)
    summed = collect_into(
        grp_index, grp_bits, lax.all_gather(group_state[None], "grp", axis=0, tiled=True)
    )
    siblings.extend([summed[bit_num] for bit_num in range(grp_bits)])
    attended = local_part(query_matrix, key_matrix, value_matrix, level_weights)
    for bit_num in range(len(siblings)):
        level_num = 1 + local_bits + bit_num
        level_scale = (level_weights[level_num] * level_factor(level_num)).T
        outer_product = jnp.einsum(
            "ryl,ylf->ryf",
            query_matrix,
            siblings[bit_num].astype(jnp.bfloat16),
            preferred_element_type=jnp.float32,
        )
        attended = attended + outer_product * level_scale[:, :, None]
    return attended.reshape(row_count, head_count * head_width).astype(jnp.bfloat16)


def solution(mesh):
    return jax.shard_map(
        on_device,
        mesh=mesh,
        in_specs=(
            P(("grp", "ctx"), None),
            P(("grp", "ctx"), None),
            P(("grp", "ctx"), None),
            P(None, None, ("grp", "ctx")),
        ),
        out_specs=P(("grp", "ctx"), None),
        check_vma=False,
    )
```

profile of v0, /device:TPU:1, one launch (start us, length us, event | category | flops | bytes accessed | tf_op | source)
XLA Modules:
  0.0 256.2 jit_solution(629913876659027636)
XLA Ops:
  6.5 0.0 copy-start
  6.5 0.0 all-gather.3.cloned.1.call-start
  6.5 1.6 copy.118
  8.2 0.5 fusion.22
  8.7 8.7 %collective-permute-start = (f32[8,128,128]{2,1,0:T(8,128)S(1)}, f32[8,128,128]{2,1,0:T(8,128)S(1)}, u32[]{:S(2)}, u32[]{:S(2)}) collective-permute-start(f32[8,128,128]{2,1,0:T(8,128)S(1)} %fusion.22), channel_id=1, source_target_pairs={{0,1},{1,0},{2,3},{3,2},{4,5},{5,4},{6,7},{7,6},{8,9},{9,8},{10,11... | collective-permute-start | bytes 1572872 | tf_op jit(solution)/shard_map/ppermute | solution.py:18
  17.4 1.5 collective-permute-done
  18.9 0.1 add.144
  19.0 1.9 collective-permute-start.1
  21.0 13.1 %collective-permute-done.1 = f32[8,128,128]{2,1,0:T(8,128)S(1)} collective-permute-done((f32[8,128,128]{2,1,0:T(8,128)S(1)}, f32[8,128,128]{2,1,0:T(8,128)S(1)}, u32[]{:S(2)}, u32[]{:S(2)}) %collective-permute-start.1) | collective-permute-done | bytes 524320 | tf_op jit(solution)/shard_map/ppermute | solution.py:18
  34.0 0.1 add.147
  34.1 0.0 copy-start.15
  34.1 2.1 collective-permute-start.2
  36.2 25.9 %collective-permute-done.2 = f32[8,128,128]{2,1,0:T(8,128)S(1)} collective-permute-done((f32[8,128,128]{2,1,0:T(8,128)S(1)}, f32[8,128,128]{2,1,0:T(8,128)S(1)}, u32[]{:S(2)}, u32[]{:S(2)}) %collective-permute-start.2) | collective-permute-done | bytes 524320 | tf_op jit(solution)/shard_map/ppermute | solution.py:18
  62.1 0.1 add.150
  62.2 3.5 %collective-permute-start.3 = (f32[8,128,128]{2,1,0:T(8,128)S(1)}, f32[8,128,128]{2,1,0:T(8,128)S(1)}, u32[]{:S(2)}, u32[]{:S(2)}) collective-permute-start(f32[8,128,128]{2,1,0:T(8,128)S(1)} %add.150), channel_id=1, source_target_pairs={{0,8},{8,0},{1,9},{9,1},{2,10},{10,2},{3,11},{11,3},{4,12},{12,4},... | collective-permute-start | bytes 1572872 | tf_op jit(solution)/shard_map/ppermute | solution.py:18
  65.7 58.6 %collective-permute-done.3 = f32[8,128,128]{2,1,0:T(8,128)S(1)} collective-permute-done((f32[8,128,128]{2,1,0:T(8,128)S(1)}, f32[8,128,128]{2,1,0:T(8,128)S(1)}, u32[]{:S(2)}, u32[]{:S(2)}) %collective-permute-start.3) | collective-permute-done | bytes 524320 | tf_op jit(solution)/shard_map/ppermute | solution.py:18
  124.2 0.1 add.153
  124.3 10.8 %collective-permute-start.4 = (f32[8,128,128]{2,1,0:T(8,128)S(1)}, f32[8,128,128]{2,1,0:T(8,128)S(1)}, u32[]{:S(2)}, u32[]{:S(2)}) collective-permute-start(f32[8,128,128]{2,1,0:T(8,128)S(1)} %add.153), channel_id=1, source_target_pairs={{0,16},{16,0},{1,17},{17,1},{2,18},{18,2},{3,19},{19,3},{4,20},{20... | collective-permute-start | bytes 1572872 | tf_op jit(solution)/shard_map/ppermute | solution.py:18
  135.1 17.5 %collective-permute-done.4 = f32[8,128,128]{2,1,0:T(8,128)S(1)} collective-permute-done((f32[8,128,128]{2,1,0:T(8,128)S(1)}, f32[8,128,128]{2,1,0:T(8,128)S(1)}, u32[]{:S(2)}, u32[]{:S(2)}) %collective-permute-start.4) | collective-permute-done | bytes 524320 | tf_op jit(solution)/shard_map/ppermute | solution.py:18
  152.6 0.0 copy-done.9
  152.6 0.8 copy-done.4
  153.5 0.8 add_convert_fusion
  154.2 0.0 all-gather.3.cloned.1.call-update
  154.3 0.6 compare_and_fusion
  154.9 0.6 compare_and_fusion.2
  155.5 0.0 copy-done.15
  155.5 0.6 multiply_bitcast_fusion.8
  156.2 1.8 fusion.47
  157.9 7.6 %fusion.2 = f32[8,512,128]{1,2,0:T(8,128)} fusion(f32[8,512]{1,0:T(8,128)} %get-tuple-element.16, f32[8,512]{1,0:T(8,128)} %get-tuple-element.17, f32[8,512]{1,0:T(8,128)} %get-tuple-element.18, f32[8,512]{1,0:T(8,128)} %get-tuple-element.19, pred[512,512]{1,0:T(8,128)(4,1)} %get-tuple-element.23, pred[512,512]{1,0:T(8,128)(4,1)} %get-tuple-element.25, ...), kind=kOutput, calls=%fused_computation.3 | convolution fusion | flops 1092616192 | bytes 6356992 | tf_op jit(solution)/shard_map/hts,shv->thv/dot_general | solution.py:46
  165.6 1.6 fusion.40
  167.2 1.9 fusion.38
  169.1 1.9 fusion.36
  170.9 1.9 fusion.34
  172.8 60.0 %all-gather.3.cloned.1.call-done = bf16[128,128,128]{2,1,0:T(8,128)(2,1)} async-done(((bf16[8,128,128]{2,1,0:T(8,128)(2,1)}), bf16[128,128,128]{2,1,0:T(8,128)(2,1)}) %all-gather.3.cloned.1.call-update) | async-done | bytes 4194320 | tf_op jit(solution)/shard_map/all_gather | solution.py:90
  232.8 0.0 copy-done.16
  232.8 4.8 %fusion.19 = bf16[4,8,128,128]{3,0,2,1:T(4,128)(2,1)S(1)} fusion(bf16[16,8,128,128]{3,2,1,0:T(8,128)(2,1)} %bitcast.192, pred[16,1]{0,1:T(4,128)(4,1)S(1)} %copy-done.16, pred[16,1]{0,1:T(4,128)(4,1)S(1)} %copy-done.17, pred[16,1]{0,1:T(4,128)(4,1)S(1)} %copy-done.18, pred[16,1]{0,1:T(4,128)(4,1)S(1)} %copy-done.19), kind=kOutput, calls=%fused_computation.31 | convolution fusion | flops 17301696 | bytes 5242944 | tf_op jit(solution)/shard_map/nl,nhkv->lhkv/dot_general | solution.py:63
  237.5 2.2 fusion.99
  239.7 0.5 fusion.31
  240.2 0.5 fusion.25
  240.7 0.5 fusion.27
  241.2 0.5 fusion.29
  241.7 0.1 copy-done.13
  241.8 0.8 copy-done.2
  242.5 0.6 copy-done.3
  243.2 0.7 copy-done.1
  243.9 0.0 copy-done.5
  243.9 3.2 %fusion.10 = bf16[512,8,128]{0,2,1:T(8,128)(2,1)} fusion(f32[8,128,512]{2,1,0:T(8,128)S(1)} %fusion.25, f32[8,128,512]{2,1,0:T(8,128)S(1)} %fusion.27, f32[8,128,512]{2,1,0:T(8,128)S(1)} %fusion.29, f32[8,128,512]{2,1,0:T(8,128)S(1)} %fusion.31, f32[8,128,512]{2,1,0:T(8,128)S(1)} %copy-done.3, f32[8,128,512]{2,1,0:T(8,128)S(1)} %copy-done.2, ...), kind=kOutput, calls=%fused_computation.11 | convolution fusion | flops 144310272 | bytes 21643264 | tf_op jit(solution)/shard_map/ryl,ylf->ryf/dot_general | solution.py:97
  247.1 2.3 copy.99
  (30 shorter events, 0.1 us)
Async XLA Ops:
  6.5 151.4 %copy-start = (bf16[512,1024]{1,0:T(8,128)(2,1)S(1)}, bf16[512,1024]{1,0:T(8,128)(2,1)}, u32[]{:S(2)}) copy-start(bf16[512,1024]{1,0:T(8,128)(2,1)} %param.4) | copy-start | bytes 3145732
  6.5 1.7 copy-start.14
  6.5 226.2 %all-gather.3.cloned.1.call-start = ((), (), s32[]{:S(2)}) async-start(), calls=%async_computation | async-start | bytes 4456448 | tf_op jit(solution)/shard_map/all_gather | solution.py:90
  8.7 10.3 %collective-permute-start = (f32[8,128,128]{2,1,0:T(8,128)S(1)}, f32[8,128,128]{2,1,0:T(8,128)S(1)}, u32[]{:S(2)}, u32[]{:S(2)}) collective-permute-start(f32[8,128,128]{2,1,0:T(8,128)S(1)} %fusion.22), channel_id=1, source_target_pairs={{0,1},{1,0},{2,3},{3,2},{4,5},{5,4},{6,7},{7,6},{8,9},{9,8},{10,11... | collective-permute-start | bytes 1572872 | tf_op jit(solution)/shard_map/ppermute | solution.py:18
  18.9 2.0 copy-start.6
  19.0 15.0 %collective-permute-start.1 = (f32[8,128,128]{2,1,0:T(8,128)S(1)}, f32[8,128,128]{2,1,0:T(8,128)S(1)}, u32[]{:S(2)}, u32[]{:S(2)}) collective-permute-start(f32[8,128,128]{2,1,0:T(8,128)S(1)} %add.144), channel_id=1, source_target_pairs={{0,2},{2,0},{1,3},{3,1},{4,6},{6,4},{5,7},{7,5},{8,10},{10,8},{9,1... | collective-permute-start | bytes 1572872 | tf_op jit(solution)/shard_map/ppermute | solution.py:18
  34.0 90.3 %copy-start.7 = (f32[8,128,128]{2,1,0:T(8,128)}, f32[8,128,128]{2,1,0:T(8,128)S(1)}, u32[]{:S(2)}) copy-start(f32[8,128,128]{2,1,0:T(8,128)S(1)} %collective-permute-done.1) | copy-start | bytes 1572868
  34.1 121.4 %copy-start.15 = (f32[13,8,512]{2,1,0:T(8,128)S(1)}, f32[13,8,512]{2,1,0:T(8,128)}, u32[]{:S(2)}) copy-start(f32[13,8,512]{2,1,0:T(8,128)} %param.7) | copy-start | bytes 638980
  34.1 28.0 %collective-permute-start.2 = (f32[8,128,128]{2,1,0:T(8,128)S(1)}, f32[8,128,128]{2,1,0:T(8,128)S(1)}, u32[]{:S(2)}, u32[]{:S(2)}) collective-permute-start(f32[8,128,128]{2,1,0:T(8,128)S(1)} %add.147), channel_id=1, source_target_pairs={{0,4},{4,0},{1,5},{5,1},{2,6},{6,2},{3,7},{7,3},{8,12},{12,8},{9,1... | collective-permute-start | bytes 1572872 | tf_op jit(solution)/shard_map/ppermute | solution.py:18
  62.1 90.5 %copy-start.9 = (f32[8,128,128]{2,1,0:T(8,128)}, f32[8,128,128]{2,1,0:T(8,128)S(1)}, u32[]{:S(2)}) copy-start(f32[8,128,128]{2,1,0:T(8,128)S(1)} %collective-permute-done.2) | copy-start | bytes 1572868
  62.2 62.1 %collective-permute-start.3 = (f32[8,128,128]{2,1,0:T(8,128)S(1)}, f32[8,128,128]{2,1,0:T(8,128)S(1)}, u32[]{:S(2)}, u32[]{:S(2)}) collective-permute-start(f32[8,128,128]{2,1,0:T(8,128)S(1)} %add.150), channel_id=1, source_target_pairs={{0,8},{8,0},{1,9},{9,1},{2,10},{10,2},{3,11},{11,3},{4,12},{12,4},... | collective-permute-start | bytes 1572872 | tf_op jit(solution)/shard_map/ppermute | solution.py:18
  124.2 28.4 %copy-start.11 = (f32[8,128,128]{2,1,0:T(8,128)}, f32[8,128,128]{2,1,0:T(8,128)S(1)}, u32[]{:S(2)}) copy-start(f32[8,128,128]{2,1,0:T(8,128)S(1)} %collective-permute-done.3) | copy-start | bytes 1572868
  124.3 28.3 %collective-permute-start.4 = (f32[8,128,128]{2,1,0:T(8,128)S(1)}, f32[8,128,128]{2,1,0:T(8,128)S(1)}, u32[]{:S(2)}, u32[]{:S(2)}) collective-permute-start(f32[8,128,128]{2,1,0:T(8,128)S(1)} %add.153), channel_id=1, source_target_pairs={{0,16},{16,0},{1,17},{17,1},{2,18},{18,2},{3,19},{19,3},{4,20},{20... | collective-permute-start | bytes 1572872 | tf_op jit(solution)/shard_map/ppermute | solution.py:18
  152.6 0.8 copy-start.4
  165.6 1.6 copy-start.8
  167.2 1.9 copy-start.10
  169.1 1.9 copy-start.12
  170.9 61.8 %copy-start.16 = (pred[16,1]{0,1:T(4,128)(4,1)S(1)}, pred[16,1]{0,1:T(4,128)(4,1)}, u32[]{:S(2)}) copy-start(pred[16,1]{0,1:T(4,128)(4,1)} %get-tuple-element.26) | copy-start | bytes 52
  170.9 61.8 %copy-start.17 = (pred[16,1]{0,1:T(4,128)(4,1)S(1)}, pred[16,1]{0,1:T(4,128)(4,1)}, u32[]{:S(2)}) copy-start(pred[16,1]{0,1:T(4,128)(4,1)} %get-tuple-element.27) | copy-start | bytes 52
  170.9 61.8 %copy-start.18 = (pred[16,1]{0,1:T(4,128)(4,1)S(1)}, pred[16,1]{0,1:T(4,128)(4,1)}, u32[]{:S(2)}) copy-start(pred[16,1]{0,1:T(4,128)(4,1)} %get-tuple-element.28) | copy-start | bytes 52
  170.9 61.8 %copy-start.19 = (pred[16,1]{0,1:T(4,128)(4,1)S(1)}, pred[16,1]{0,1:T(4,128)(4,1)}, u32[]{:S(2)}) copy-start(pred[16,1]{0,1:T(4,128)(4,1)} %get-tuple-element.29) | copy-start | bytes 52
  240.2 1.6 copy-start.13
  240.7 1.8 copy-start.2
  240.7 2.5 copy-start.3
  241.2 2.7 %copy-start.1 = (f32[8,128,512]{2,1,0:T(8,128)S(1)}, f32[8,128,512]{2,1,0:T(8,128)}, u32[]{:S(2)}) copy-start(f32[8,128,512]{2,1,0:T(8,128)} %fusion.38) | copy-start | bytes 6291460
  241.2 2.7 %copy-start.5 = (f32[8,128,128]{2,1,0:T(8,128)S(1)}, f32[8,128,128]{2,1,0:T(8,128)}, u32[]{:S(2)}) copy-start(f32[8,128,128]{2,1,0:T(8,128)} %copy-done.4) | copy-start | bytes 1572868
Sparse Core Ops, SparseCore 0:
  154.4 78.3 all-gather.2
where the time goes:
time: 257 us; the launch traced here: 256 us
  waiting for transfers between devices  177 us (69%)
  starting transfers between devices  27 us (11%)
  matrix products  25.2 us (10%)
  between operations  13.7 us (5%)
  local copies, waits for them, and re-layouts  9.12 us (4%)
  other arithmetic  4.59 us (2%)
    ppermute x5, waiting for transfers between devices, from_partner(): return lax.ppermute(block, axis, route)  117 us
    all_gather x1, waiting for transfers between devices, on_device(): lax.all_gather(group_state[None], 'grp', axis=0, tiled=True)  60 us
    ppermute x5, starting transfers between devices, from_partner(): return lax.ppermute(block, axis, route)  27 us
    dot_general x9, matrix products, on_device(): jnp.einsum('ryl,ylf->ryf', query_matrix, siblings[bit_num].astype(jnp.bfl...  12.3 us
    dot_general x1, matrix products, local_part(): jnp.einsum('hts,shv->thv', weighted, value_matrix, preferred_element_type...  7.63 us
  transfers between devices with their start and end apart: 6, of which 6 were waited for; matrix products, arithmetic and copies ran while one was open for 7% of the time, Pallas kernels for 0%

commit v1 on v0

--- a/solution.py
+++ b/solution.py
@@ -87,7 +87,12 @@
         running = running + partner
     group_state = running.astype(jnp.bfloat16)
     summed = collect_into(
-        grp_index, grp_bits, lax.all_gather(group_state[None], "grp", axis=0, tiled=True)
+        grp_index,
+        grp_bits,
+        jnp.concatenate(
+            lax.all_to_all(jnp.stack([group_state[None]] * lax.axis_size("grp")), "grp", 0, 0),
+            axis=0,
+        ),
     )
     siblings.extend([summed[bit_num] for bit_num in range(grp_bits)])
     attended = local_part(query_matrix, key_matrix, value_matrix, level_weights)

time: 257 us -> 247 us (0.961)
  the two profiles are of different devices: /device:TPU:1 before, /device:TPU:96 now
where the time goes in v1:
time: 247 us
  waiting for transfers between devices  171 us (69%)
  starting transfers between devices  34.5 us (14%)
  matrix products  23.9 us (10%)
  local copies, waits for them, and re-layouts  12.8 us (5%)
  other arithmetic  3.82 us (2%)
    ppermute x5, waiting for transfers between devices, from_partner(): return lax.ppermute(block, axis, route)  126 us
    all_to_all x1, waiting for transfers between devices, on_device(): lax.all_to_all(jnp.stack([group_state[None]] * lax.axis_size('grp')), 'gr...  45.7 us
    ppermute x5, starting transfers between devices, from_partner(): return lax.ppermute(block, axis, route)  27.6 us
    dot_general x9, matrix products, on_device(): jnp.einsum('ryl,ylf->ryf', query_matrix, siblings[bit_num].astype(jnp.bfl...  11.1 us
    dot_general x1, matrix products, local_part(): jnp.einsum('hts,shv->thv', weighted, value_matrix, preferred_element_type...  7.63 us
    all_to_all x1, starting transfers between devices, on_device(): lax.all_to_all(jnp.stack([group_state[None]] * lax.axis_size('grp')), 'gr...  6.94 us
  transfers between devices with their start and end apart: 6, of which 6 were waited for; matrix products, arithmetic and copies ran while one was open for 7% of the time, Pallas kernels for 0%

profile of v1, /device:TPU:96, one launch (start us, length us, event | category | flops | bytes accessed | tf_op | source)
XLA Modules:
  0.0 246.7 jit_solution(402290822007762026)
XLA Ops:
  0.0 1.6 copy.92
  1.7 0.5 fusion.23
  2.1 1.9 collective-permute-start
  4.1 1.9 collective-permute-done
  5.9 0.1 add.144
  6.0 2.0 collective-permute-start.1
  8.1 13.8 %collective-permute-done.1 = f32[8,128,128]{2,1,0:T(8,128)S(1)} collective-permute-done((f32[8,128,128]{2,1,0:T(8,128)S(1)}, f32[8,128,128]{2,1,0:T(8,128)S(1)}, u32[]{:S(2)}, u32[]{:S(2)}) %collective-permute-start.1) | collective-permute-done | bytes 524320 | tf_op jit(solution)/shard_map/ppermute | solution.py:18
  21.9 0.1 add.147
  21.9 5.3 %collective-permute-start.2 = (f32[8,128,128]{2,1,0:T(8,128)S(1)}, f32[8,128,128]{2,1,0:T(8,128)S(1)}, u32[]{:S(2)}, u32[]{:S(2)}) collective-permute-start(f32[8,128,128]{2,1,0:T(8,128)S(1)} %add.147), channel_id=1, source_target_pairs={{0,4},{4,0},{1,5},{5,1},{2,6},{6,2},{3,7},{7,3},{8,12},{12,8},{9,1... | collective-permute-start | bytes 1572872 | tf_op jit(solution)/shard_map/ppermute | solution.py:18
  27.2 22.9 %collective-permute-done.2 = f32[8,128,128]{2,1,0:T(8,128)S(1)} collective-permute-done((f32[8,128,128]{2,1,0:T(8,128)S(1)}, f32[8,128,128]{2,1,0:T(8,128)S(1)}, u32[]{:S(2)}, u32[]{:S(2)}) %collective-permute-start.2) | collective-permute-done | bytes 524320 | tf_op jit(solution)/shard_map/ppermute | solution.py:18
  50.1 0.1 add.150
  50.2 8.0 %collective-permute-start.3 = (f32[8,128,128]{2,1,0:T(8,128)S(1)}, f32[8,128,128]{2,1,0:T(8,128)S(1)}, u32[]{:S(2)}, u32[]{:S(2)}) collective-permute-start(f32[8,128,128]{2,1,0:T(8,128)S(1)} %add.150), channel_id=1, source_target_pairs={{0,8},{8,0},{1,9},{9,1},{2,10},{10,2},{3,11},{11,3},{4,12},{12,4},... | collective-permute-start | bytes 1572872 | tf_op jit(solution)/shard_map/ppermute | solution.py:18
  58.2 52.4 %collective-permute-done.3 = f32[8,128,128]{2,1,0:T(8,128)S(1)} collective-permute-done((f32[8,128,128]{2,1,0:T(8,128)S(1)}, f32[8,128,128]{2,1,0:T(8,128)S(1)}, u32[]{:S(2)}, u32[]{:S(2)}) %collective-permute-start.3) | collective-permute-done | bytes 524320 | tf_op jit(solution)/shard_map/ppermute | solution.py:18
  110.5 0.1 add.153
  110.6 0.0 copy-done.7
  110.6 10.4 %collective-permute-start.4 = (f32[8,128,128]{2,1,0:T(8,128)S(1)}, f32[8,128,128]{2,1,0:T(8,128)S(1)}, u32[]{:S(2)}, u32[]{:S(2)}) collective-permute-start(f32[8,128,128]{2,1,0:T(8,128)S(1)} %add.153), channel_id=1, source_target_pairs={{0,16},{16,0},{1,17},{17,1},{2,18},{18,2},{3,19},{19,3},{4,20},{20... | collective-permute-start | bytes 1572872 | tf_op jit(solution)/shard_map/ppermute | solution.py:18
  121.0 34.7 %collective-permute-done.4 = f32[8,128,128]{2,1,0:T(8,128)S(1)} collective-permute-done((f32[8,128,128]{2,1,0:T(8,128)S(1)}, f32[8,128,128]{2,1,0:T(8,128)S(1)}, u32[]{:S(2)}, u32[]{:S(2)}) %collective-permute-start.4) | collective-permute-done | bytes 524320 | tf_op jit(solution)/shard_map/ppermute | solution.py:18
  155.7 0.0 copy-done.9
  155.7 0.8 copy-done.4
  156.5 0.1 add_convert_fusion
  156.6 3.1 %stack.5 = bf16[16,1,8,128,128]{4,3,2,1,0:T(8,128)(2,1)} broadcast(bf16[8,128,128]{2,1,0:T(8,128)(2,1)S(1)} %add_convert_fusion), dimensions={2,3,4} | broadcast | bytes 4456448 | tf_op jit(solution)/shard_map/stack | solution.py:93
  159.6 6.9 %all-to-all-start = ((bf16[16,1,8,128,128]{4,3,2,1,0:T(8,128)(2,1)}), bf16[16,1,8,128,128]{4,3,2,1,0:T(8,128)(2,1)}, u32[]{:S(2)}, u32[]{:S(2)}) async-start(bf16[16,1,8,128,128]{4,3,2,1,0:T(8,128)(2,1)} %stack.5), calls=%async_computation | async-start | bytes 8388608 | tf_op jit(solution)/shard_map/all_to_all | solution.py:93
  166.7 0.6 compare_and_fusion
  167.3 0.6 compare_and_fusion.2
  167.9 0.6 multiply_bitcast_fusion.8
  168.5 1.7 fusion.48
  170.2 7.6 %fusion.3 = f32[8,512,128]{1,2,0:T(8,128)} fusion(f32[8,512]{1,0:T(8,128)} %get-tuple-element.16, f32[8,512]{1,0:T(8,128)} %get-tuple-element.17, f32[8,512]{1,0:T(8,128)} %get-tuple-element.18, f32[8,512]{1,0:T(8,128)} %get-tuple-element.19, pred[512,512]{1,0:T(8,128)(4,1)} %get-tuple-element.23, pred[512,512]{1,0:T(8,128)(4,1)} %get-tuple-element.25, ...), kind=kOutput, calls=%fused_computation.4 | convolution fusion | flops 1092616192 | bytes 6356992 | tf_op jit(solution)/shard_map/hts,shv->thv/dot_general | solution.py:46
  177.8 0.5 fusion.41
  178.3 0.5 copy-done.8
  178.9 1.8 fusion.39
  180.7 0.0 copy-done.10
  180.7 1.8 fusion.37
  182.5 1.8 fusion.35
  184.3 45.7 %all-to-all-done = bf16[16,1,8,128,128]{4,3,2,1,0:T(8,128)(2,1)} async-done(((bf16[16,1,8,128,128]{4,3,2,1,0:T(8,128)(2,1)}), bf16[16,1,8,128,128]{4,3,2,1,0:T(8,128)(2,1)}, u32[]{:S(2)}, u32[]{:S(2)}) %all-to-all-start) | async-done | bytes 4194336 | tf_op jit(solution)/shard_map/all_to_all | solution.py:93
  230.0 4.8 %fusion.20 = bf16[4,8,128,128]{3,0,2,1:T(4,128)(2,1)S(1)} fusion(bf16[16,1,8,128,128]{4,3,2,1,0:T(8,128)(2,1)} %all-to-all-done, pred[16,1]{0,1:T(4,128)(4,1)S(1)} %copy-done.16, pred[16,1]{0,1:T(4,128)(4,1)S(1)} %copy-done.17, pred[16,1]{0,1:T(4,128)(4,1)S(1)} %copy-done.18, pred[16,1]{0,1:T(4,128)(4,1)S(1)} %copy-done.19), kind=kOutput, calls=%fused_computation.32 | convolution fusion | flops 17301696 | bytes 5242944 | tf_op jit(solution)/shard_map/nl,nhkv->lhkv/dot_general | solution.py:63
  234.8 2.2 fusion.100
  237.0 0.5 fusion.32
  237.5 0.0 copy-start.13
  237.5 0.5 fusion.26
  238.0 0.5 fusion.28
  238.5 0.5 fusion.30
  239.0 0.1 copy-done.13
  239.1 0.8 copy-done.2
  239.9 0.6 copy-done.3
  240.5 0.7 copy-done.1
  241.2 0.0 copy-done.5
  241.2 3.2 %fusion.11 = bf16[512,8,128]{0,2,1:T(8,128)(2,1)} fusion(f32[8,128,512]{2,1,0:T(8,128)S(1)} %fusion.26, f32[8,128,512]{2,1,0:T(8,128)S(1)} %fusion.28, f32[8,128,512]{2,1,0:T(8,128)S(1)} %fusion.30, f32[8,128,512]{2,1,0:T(8,128)S(1)} %fusion.32, f32[8,128,512]{2,1,0:T(8,128)S(1)} %copy-done.3, f32[8,128,512]{2,1,0:T(8,128)S(1)} %copy-done.2, ...), kind=kOutput, calls=%fused_computation.12 | convolution fusion | flops 144310272 | bytes 21643264 | tf_op jit(solution)/shard_map/ryl,ylf->ryf/dot_general | solution.py:102
  244.4 2.3 copy.73
  (30 shorter events, 0.1 us)
Async XLA Ops:
  0.0 170.2 %copy-start = (bf16[512,1024]{1,0:T(8,128)(2,1)S(1)}, bf16[512,1024]{1,0:T(8,128)(2,1)}, u32[]{:S(2)}) copy-start(bf16[512,1024]{1,0:T(8,128)(2,1)} %param.4) | copy-start | bytes 3145732
  0.0 1.7 copy-start.14
  2.1 3.8 %collective-permute-start = (f32[8,128,128]{2,1,0:T(8,128)S(1)}, f32[8,128,128]{2,1,0:T(8,128)S(1)}, u32[]{:S(2)}, u32[]{:S(2)}) collective-permute-start(f32[8,128,128]{2,1,0:T(8,128)S(1)} %fusion.23), channel_id=1, source_target_pairs={{0,1},{1,0},{2,3},{3,2},{4,5},{5,4},{6,7},{7,6},{8,9},{9,8},{10,11... | collective-permute-start | bytes 1572872 | tf_op jit(solution)/shard_map/ppermute | solution.py:18
  5.9 2.1 copy-start.6
  6.0 15.9 %collective-permute-start.1 = (f32[8,128,128]{2,1,0:T(8,128)S(1)}, f32[8,128,128]{2,1,0:T(8,128)S(1)}, u32[]{:S(2)}, u32[]{:S(2)}) collective-permute-start(f32[8,128,128]{2,1,0:T(8,128)S(1)} %add.144), channel_id=1, source_target_pairs={{0,2},{2,0},{1,3},{3,1},{4,6},{6,4},{5,7},{7,5},{8,10},{10,8},{9,1... | collective-permute-start | bytes 1572872 | tf_op jit(solution)/shard_map/ppermute | solution.py:18
  21.9 88.7 %copy-start.7 = (f32[8,128,128]{2,1,0:T(8,128)}, f32[8,128,128]{2,1,0:T(8,128)S(1)}, u32[]{:S(2)}) copy-start(f32[8,128,128]{2,1,0:T(8,128)S(1)} %collective-permute-done.1) | copy-start | bytes 1572868
  21.9 28.2 %collective-permute-start.2 = (f32[8,128,128]{2,1,0:T(8,128)S(1)}, f32[8,128,128]{2,1,0:T(8,128)S(1)}, u32[]{:S(2)}, u32[]{:S(2)}) collective-permute-start(f32[8,128,128]{2,1,0:T(8,128)S(1)} %add.147), channel_id=1, source_target_pairs={{0,4},{4,0},{1,5},{5,1},{2,6},{6,2},{3,7},{7,3},{8,12},{12,8},{9,1... | collective-permute-start | bytes 1572872 | tf_op jit(solution)/shard_map/ppermute | solution.py:18
  50.1 105.6 %copy-start.9 = (f32[8,128,128]{2,1,0:T(8,128)}, f32[8,128,128]{2,1,0:T(8,128)S(1)}, u32[]{:S(2)}) copy-start(f32[8,128,128]{2,1,0:T(8,128)S(1)} %collective-permute-done.2) | copy-start | bytes 1572868
  50.2 60.4 %collective-permute-start.3 = (f32[8,128,128]{2,1,0:T(8,128)S(1)}, f32[8,128,128]{2,1,0:T(8,128)S(1)}, u32[]{:S(2)}, u32[]{:S(2)}) collective-permute-start(f32[8,128,128]{2,1,0:T(8,128)S(1)} %add.150), channel_id=1, source_target_pairs={{0,8},{8,0},{1,9},{9,1},{2,10},{10,2},{3,11},{11,3},{4,12},{12,4},... | collective-permute-start | bytes 1572872 | tf_op jit(solution)/shard_map/ppermute | solution.py:18
  110.5 45.2 %copy-start.11 = (f32[8,128,128]{2,1,0:T(8,128)}, f32[8,128,128]{2,1,0:T(8,128)S(1)}, u32[]{:S(2)}) copy-start(f32[8,128,128]{2,1,0:T(8,128)S(1)} %collective-permute-done.3) | copy-start | bytes 1572868
  110.6 45.1 %collective-permute-start.4 = (f32[8,128,128]{2,1,0:T(8,128)S(1)}, f32[8,128,128]{2,1,0:T(8,128)S(1)}, u32[]{:S(2)}, u32[]{:S(2)}) collective-permute-start(f32[8,128,128]{2,1,0:T(8,128)S(1)} %add.153), channel_id=1, source_target_pairs={{0,16},{16,0},{1,17},{17,1},{2,18},{18,2},{3,19},{19,3},{4,20},{20... | collective-permute-start | bytes 1572872 | tf_op jit(solution)/shard_map/ppermute | solution.py:18
  155.7 0.8 copy-start.4
  159.6 8.2 %copy-start.15 = (f32[13,8,512]{2,1,0:T(8,128)S(1)}, f32[13,8,512]{2,1,0:T(8,128)}, u32[]{:S(2)}) copy-start(f32[13,8,512]{2,1,0:T(8,128)} %param.7) | copy-start | bytes 638980
  159.6 70.4 %all-to-all-start = ((bf16[16,1,8,128,128]{4,3,2,1,0:T(8,128)(2,1)}), bf16[16,1,8,128,128]{4,3,2,1,0:T(8,128)(2,1)}, u32[]{:S(2)}, u32[]{:S(2)}) async-start(bf16[16,1,8,128,128]{4,3,2,1,0:T(8,128)(2,1)} %stack.5), calls=%async_computation | async-start | bytes 8388608 | tf_op jit(solution)/shard_map/all_to_all | solution.py:93
  177.8 1.0 copy-start.8
  178.9 1.8 copy-start.10
  180.7 1.8 copy-start.12
  182.5 47.5 %copy-start.16 = (pred[16,1]{0,1:T(4,128)(4,1)S(1)}, pred[16,1]{0,1:T(4,128)(4,1)}, u32[]{:S(2)}) copy-start(pred[16,1]{0,1:T(4,128)(4,1)} %get-tuple-element.26) | copy-start | bytes 52
  182.5 47.5 %copy-start.17 = (pred[16,1]{0,1:T(4,128)(4,1)S(1)}, pred[16,1]{0,1:T(4,128)(4,1)}, u32[]{:S(2)}) copy-start(pred[16,1]{0,1:T(4,128)(4,1)} %get-tuple-element.27) | copy-start | bytes 52
  182.5 47.5 %copy-start.18 = (pred[16,1]{0,1:T(4,128)(4,1)S(1)}, pred[16,1]{0,1:T(4,128)(4,1)}, u32[]{:S(2)}) copy-start(pred[16,1]{0,1:T(4,128)(4,1)} %get-tuple-element.28) | copy-start | bytes 52
  182.5 47.5 %copy-start.19 = (pred[16,1]{0,1:T(4,128)(4,1)S(1)}, pred[16,1]{0,1:T(4,128)(4,1)}, u32[]{:S(2)}) copy-start(pred[16,1]{0,1:T(4,128)(4,1)} %get-tuple-element.29) | copy-start | bytes 52
  237.5 1.6 copy-start.13
  238.0 1.8 copy-start.2
  238.0 2.5 %copy-start.3 = (f32[8,128,512]{2,1,0:T(8,128)S(1)}, f32[8,128,512]{2,1,0:T(8,128)}, u32[]{:S(2)}) copy-start(f32[8,128,512]{2,1,0:T(8,128)} %fusion.35) | copy-start | bytes 6291460
  238.5 2.7 %copy-start.1 = (f32[8,128,512]{2,1,0:T(8,128)S(1)}, f32[8,128,512]{2,1,0:T(8,128)}, u32[]{:S(2)}) copy-start(f32[8,128,512]{2,1,0:T(8,128)} %fusion.39) | copy-start | bytes 6291460
  238.5 2.7 %copy-start.5 = (f32[8,128,128]{2,1,0:T(8,128)S(1)}, f32[8,128,128]{2,1,0:T(8,128)}, u32[]{:S(2)}) copy-start(f32[8,128,128]{2,1,0:T(8,128)} %copy-done.4) | copy-start | bytes 1572868
